TPU v7x, 32 devices: a whole 2x2x4 slice. The times are simulated.
32 devices in a mesh: groups: 2 (over x), wide: 16 (over z, y, core).
Axes of the slice: x: 2, y: 2, z: 4, core: 2. Of those that a mesh axis runs over, the one named last changes fastest.
Arguments:
- prefix_hidden: bfloat16 [32, 256, 8192], P(('groups', 'wide')), parts along dimension 0, may hold values from -6 to 6
- prefix_lengths: int32 [32], P(('groups', 'wide')), parts along dimension 0, may hold values from 64 to 256
- action_noise: float32 [32, 50, 32], P(('groups', 'wide')), parts along dimension 0, may hold values from -4 to 4
- prefix_gain: float32 [8192], replicated, may hold values from 0.1 to 1.9
- key_weight: bfloat16 [8192, 512], P('wide'), may hold values from -0.0625 to 0.0625
- value_weight: bfloat16 [8192, 512], P('wide'), may hold values from -0.0625 to 0.0625
- input_weight: float32 [32, 1024], replicated, may hold values from -1 to 1
- expert_gain: float32 [1024], replicated, may hold values from 0.1 to 1.9
- expert_query: bfloat16 [1024, 1024], P('wide'), may hold values from -0.1875 to 0.1875
- expert_key: bfloat16 [1024, 512], P('wide'), may hold values from -5.3125 to 5.3125
- expert_value: bfloat16 [1024, 512], P('wide'), may hold values from -0.1875 to 0.1875
- expert_output: bfloat16 [1024, 1024], P('wide'), may hold values from -0.1875 to 0.1875
- final_gain: float32 [1024], replicated, may hold values from 0.1 to 1.9
- output_weight: bfloat16 [1024, 32], replicated, may hold values from -0.1875 to 0.1875
Outputs:
- actions: float32 [32, 50, 32], P(('groups', 'wide')), parts along dimension 0
There are 2 independent parts, one for each index of `groups`. A program takes and returns all parts, laid end to end along the dimension named above; an argument that names none is the same for every part. Nothing has to cross between parts.
Inputs may be any that keep to these rules, and one draw needn't show every extreme that they name: `prefix_lengths`: positions at or after a sample's length are padding and take no part.
All inputs are finite; a program needn't handle non-finite values.
Results may differ from a plain program's by a relative error of at most 0.0075.
Values may be sent and summed in bfloat16 or wider, within the bound.
A program may use at most 128 MiB of HBM per device.

v0:
```python
import jax
import jax.numpy as jnp
from jax import lax
from jax.sharding import PartitionSpec as P

HEAD = 128
STEPS = 4
rope_base = 1000000.0
norm_eps = 1e-06


def normalize(values, norm_gain):
    mean_square = jnp.mean(values * values, axis=-1, keepdims=True)
    return values * lax.rsqrt(mean_square + norm_eps) * norm_gain


def rotate(values, positions):
    half_width = values.shape[-1] // 2
    inv_freqs = rope_base ** (-jnp.arange(half_width, dtype=jnp.float32) * 2.0 / values.shape[-1])
    angles = positions[:, None] * inv_freqs[None, :]
    cosine = jnp.cos(angles)[:, None, :]
    sine_part = jnp.sin(angles)[:, None, :]
    first_half = values[..., :half_width]
    second = values[..., half_width:]
    return jnp.concatenate(
        [first_half * cosine - second * sine_part, second * cosine + first_half * sine_part], -1
    )


def time_embedding(time_value, embed_width):
    half_width = embed_width // 2
    fraction = jnp.arange(half_width, dtype=jnp.float32) / (half_width - 1)
    period = 0.004 * (4.0 / 0.004) ** fraction
    angles = time_value * (2.0 * jnp.pi) / period
    return jnp.concatenate([jnp.sin(angles), jnp.cos(angles)])


def attend(queries, key_cache, value_cache, action_keys, action_values, is_valid):
    span_rows = queries.shape[0]
    groups = key_cache.shape[1] // HEAD
    group_ratio = queries.shape[1] // key_cache.shape[1]
    query_heads = queries.reshape(span_rows, groups, group_ratio, HEAD)
    prefix_keys = key_cache.reshape(-1, groups, HEAD)
    prefix_values = value_cache.reshape(-1, groups, HEAD)
    own_keys = action_keys.reshape(span_rows, groups, HEAD)
    own_values = action_values.reshape(span_rows, groups, HEAD)
    prefix_scores = jnp.einsum(
        "cgrh,pgh->grcp", query_heads, prefix_keys, preferred_element_type=jnp.float32
    )
    prefix_scores = jnp.where(is_valid[None, None, None, :], prefix_scores, -1e30)
    own_scores = jnp.einsum(
        "cgrh,ngh->grcn", query_heads, own_keys, preferred_element_type=jnp.float32
    )
    row_max = jnp.maximum(jnp.max(prefix_scores, -1), jnp.max(own_scores, -1))[..., None]
    prefix_exp = jnp.exp(prefix_scores - row_max)
    own_exp = jnp.exp(own_scores - row_max)
    prob_total = jnp.sum(prefix_exp, -1, keepdims=True) + jnp.sum(own_exp, -1, keepdims=True)
    prefix_prob = (prefix_exp / prob_total).astype(jnp.bfloat16)
    own_prob = (own_exp / prob_total).astype(jnp.bfloat16)
    attn_mixed = jnp.einsum(
        "grcp,pgh->cgrh", prefix_prob, prefix_values, preferred_element_type=jnp.float32
    )
    attn_mixed = attn_mixed + jnp.einsum(
        "grcn,ngh->cgrh", own_prob, own_values, preferred_element_type=jnp.float32
    )
    return attn_mixed.reshape(span_rows, -1).astype(jnp.bfloat16)


def expert_steps(
    noise_rows,
    length,
    input_weight,
    expert_gain,
    query_w,
    key_w,
    value_w,
    output_w,
    final_gain,
    output_weight,
    key_cache,
    value_cache,
):
    span_rows = noise_rows.shape[0]
    is_valid = jnp.arange(key_cache.shape[0], dtype=jnp.int32) < length
    positions = length.astype(jnp.float32) + jnp.arange(span_rows, dtype=jnp.float32)
    action_state = noise_rows
    for step_idx in range(STEPS):
        time_value = 1.0 - step_idx / STEPS
        hidden = jnp.dot(
            action_state,
            input_weight,
            precision=lax.Precision.HIGHEST,
            preferred_element_type=jnp.float32,
        )
        hidden = hidden + time_embedding(time_value, input_weight.shape[1])[None, :]
        normed = normalize(hidden, expert_gain).astype(jnp.bfloat16)
        raw_queries = jnp.dot(normed, query_w, preferred_element_type=jnp.float32)
        queries = rotate(raw_queries.reshape(span_rows, -1, HEAD), positions).reshape(span_rows, -1)
        queries = (queries * HEAD ** (-0.5)).astype(jnp.bfloat16)
        raw_keys = jnp.dot(normed, key_w, preferred_element_type=jnp.float32)
        action_keys = (
            rotate(raw_keys.reshape(span_rows, -1, HEAD), positions)
            .reshape(span_rows, -1)
            .astype(jnp.bfloat16)
        )
        action_values = jnp.dot(normed, value_w, preferred_element_type=jnp.float32).astype(
            jnp.bfloat16
        )
        attn_mixed = attend(queries, key_cache, value_cache, action_keys, action_values, is_valid)
        hidden = hidden + jnp.dot(attn_mixed, output_w, preferred_element_type=jnp.float32)
        final_normed = normalize(hidden, final_gain).astype(jnp.bfloat16)
        velocity = jnp.dot(final_normed, output_weight, preferred_element_type=jnp.float32)
        action_state = action_state - velocity / STEPS
    return action_state


def shards(
    prefix_hidden,
    prefix_lengths,
    action_noise,
    prefix_gain,
    key_weight,
    value_weight,
    input_weight,
    expert_gain,
    expert_query,
    expert_key,
    expert_value,
    expert_output,
    final_gain,
    output_weight,
):
    gathered = (
        lax.all_gather(expert_query, "wide", axis=0, tiled=True),
        lax.all_gather(expert_key, "wide", axis=0, tiled=True),
        lax.all_gather(expert_value, "wide", axis=0, tiled=True),
        lax.all_gather(expert_output, "wide", axis=0, tiled=True),
    )
    hidden = prefix_hidden[0]
    row_count = hidden.shape[0]
    normed = normalize(hidden.astype(jnp.float32), prefix_gain).astype(jnp.bfloat16)
    stacked = jnp.stack([key_weight, value_weight], 0)
    projected = jnp.einsum(
        "pd,kdc->pkc",
        normed,
        lax.all_gather(stacked, "wide", axis=1, tiled=True),
        preferred_element_type=jnp.float32,
    )
    positions = jnp.arange(row_count, dtype=jnp.float32)
    key_cache = (
        rotate(projected[:, 0].reshape(row_count, -1, HEAD), positions)
        .reshape(row_count, -1)
        .astype(jnp.bfloat16)
    )
    value_cache = projected[:, 1].astype(jnp.bfloat16)
    query_w, key_w, value_w, output_w = gathered
    action_state = expert_steps(
        action_noise[0],
        prefix_lengths[0],
        input_weight,
        expert_gain,
        query_w,
        key_w,
        value_w,
        output_w,
        final_gain,
        output_weight,
        key_cache,
        value_cache,
    )
    return action_state[None]


def solution(mesh):
    placed = (
        P(("groups", "wide"), None, None),
        P(("groups", "wide")),
        P(("groups", "wide"), None, None),
        P(),
        P("wide", None),
        P("wide", None),
        P(),
        P(),
        P("wide", None),
        P("wide", None),
        P("wide", None),
        P("wide", None),
        P(),
        P(),
    )
    return jax.shard_map(
        shards,
        mesh=mesh,
        in_specs=placed,
        out_specs=P(("groups", "wide"), None, None),
        check_vma=False,
    )
```

profile of v0, /device:TPU:0, one launch (start us, length us, event | category | flops | bytes accessed | tf_op | source)
XLA Modules:
  0.0 368.0 jit_solution(7898720133912089493)
XLA Ops:
  6.5 0.7 all-gather.10.cloned.1.call-update
  7.3 0.7 all-gather.12.cloned.1.call-update
  8.1 0.7 all-gather.8.cloned.1.call-update
  8.8 2.3 pad_maximum_fusion
  11.1 0.5 all-gather.14.cloned.1.call-update
  12.0 3.1 fusion
  15.1 0.5 fusion.47
  17.1 0.6 pad_maximum_fusion.2
  17.7 0.6 pad_maximum_fusion.3
  18.3 0.6 pad_maximum_fusion.4
  19.0 31.2 %all-gather.10.cloned.1.call-done = bf16[1024,512]{1,0:T(8,128)(2,1)} async-done(((bf16[64,512]{1,0:T(8,128)(2,1)}), bf16[1024,512]{1,0:T(8,128)(2,1)}) %all-gather.10.cloned.1.call-update) | async-done | bytes 1048592 | tf_op jit(solution)/shard_map/all_gather | solution.py:135
  50.2 1.5 fusion.107
  51.9 37.4 %all-gather.12.cloned.1.call-done = bf16[1024,512]{1,0:T(8,128)(2,1)} async-done(((bf16[64,512]{1,0:T(8,128)(2,1)}), bf16[1024,512]{1,0:T(8,128)(2,1)}) %all-gather.12.cloned.1.call-update) | async-done | bytes 1048592 | tf_op jit(solution)/shard_map/all_gather | solution.py:136
  89.2 1.5 convolution_convert_fusion.3
  90.7 0.6 reshape.309
  91.4 40.4 %all-gather.8.cloned.1.call-done = bf16[1024,1024]{1,0:T(8,128)(2,1)} async-done(((bf16[64,1024]{1,0:T(8,128)(2,1)}), bf16[1024,1024]{1,0:T(8,128)(2,1)}) %all-gather.8.cloned.1.call-update) | async-done | bytes 2097168 | tf_op jit(solution)/shard_map/all_gather | solution.py:134
  131.9 2.1 fusion.106
  134.6 124.5 %all-gather.6.cloned.1.call-done = bf16[2,8192,512]{2,1,0:T(8,128)(2,1)} async-done(((bf16[2,512,512]{2,1,0:T(8,128)(2,1)}), bf16[2,8192,512]{2,1,0:T(8,128)(2,1)}) %all-gather.6.cloned.1.call-update) | async-done | bytes 16777232 | tf_op jit(solution)/shard_map/all_gather | solution.py:146
  259.1 9.5 %fusion.4 = f32[256,2,512]{2,0,1:T(8,128)S(1)} fusion(bf16[2,8192,512]{2,1,0:T(8,128)(2,1)} %all-gather.6.cloned.1.call-done, bf16[1,256,8192]{2,1,0:T(8,128)(2,1)} %param.14, f32[8192]{0:T(1024)S(1)} %copy-done.58, f32[256]{0:T(256)S(1)} %add_rsqrt_fusion), kind=kOutput, calls=%fused_computation.6 | convolution fusion | flops 4303355904 | bytes 22053888 | tf_op jit(solution)/shard_map/pd,kdc->pkc/dot_general | solution.py:143
  271.2 29.5 %all-gather.14.cloned.1.call-done = bf16[1024,1024]{1,0:T(8,128)(2,1)} async-done(((bf16[64,1024]{1,0:T(8,128)(2,1)}), bf16[1024,1024]{1,0:T(8,128)(2,1)}) %all-gather.14.cloned.1.call-update) | async-done | bytes 2097168 | tf_op jit(solution)/shard_map/all_gather | solution.py:137
  300.8 2.2 multiply_reduce_fusion.6
  303.9 0.6 copy-done.21
  305.3 0.6 copy-done.34
  306.0 1.7 fusion.100
  307.7 0.9 fusion.109
  308.6 1.6 reshape.311
  310.2 1.1 fusion.96
  311.3 0.8 subtract_convert_fusion.3
  312.1 1.2 fusion.101
  313.3 0.7 max.29
  314.1 1.3 fusion.27
  315.5 2.1 fusion.31
  317.6 0.9 convolution_convert_fusion.2
  318.5 1.5 reshape.312
  320.0 1.3 fusion.19
  321.3 0.7 copy.50
  322.0 1.6 convert_element_type.174
  323.6 2.2 multiply_reduce_fusion.4
  326.7 0.7 copy-done.22
  328.4 0.6 copy-done.35
  329.0 1.1 fusion.102
  330.1 0.9 fusion.111
  331.1 1.6 reshape.314
  332.6 1.1 fusion.95
  333.7 0.8 subtract_convert_fusion.2
  334.5 1.2 fusion.103
  335.7 1.4 fusion.28
  337.2 2.1 fusion.32
  339.3 0.9 convolution_convert_fusion.1
  340.2 1.5 reshape.315
  341.7 1.3 fusion.18
  343.0 0.7 copy.57
  343.7 1.6 convert_element_type.184
  345.3 2.2 multiply_reduce_fusion.2
  347.6 1.0 fusion.23
  348.6 1.2 multiply_reduce_fusion.1
  349.8 0.7 copy-done.19
  350.5 0.8 multiply_convert_fusion.1
  354.5 2.3 fusion.33
  356.7 0.9 convolution_convert_fusion
  357.7 0.9 reshape.318
  358.5 1.3 fusion.17
  360.0 0.6 multiply_reduce_fusion
  360.6 0.8 fusion.22
  (205 shorter events, 11.1 us)
Async XLA Ops:
  6.5 9.1 %copy-start = (f32[32,1024]{1,0:T(8,128)S(1)}, f32[32,1024]{1,0:T(8,128)}, u32[]{:S(2)}) copy-start(f32[32,1024]{1,0:T(8,128)} %param.20) | copy-start | bytes 393220
  6.5 43.7 %all-gather.10.cloned.1.call-start = ((), (), s32[]{:S(2)}) async-start(), calls=%async_computation.2 | async-start | bytes 1114112 | tf_op jit(solution)/shard_map/all_gather | solution.py:135
  7.3 82.0 %all-gather.12.cloned.1.call-start = ((), (), s32[]{:S(2)}) async-start(), calls=%async_computation.3 | async-start | bytes 1114112 | tf_op jit(solution)/shard_map/all_gather | solution.py:136
  8.0 123.8 %all-gather.8.cloned.1.call-start = ((), (), s32[]{:S(2)}) async-start(), calls=%async_computation.1 | async-start | bytes 2228224 | tf_op jit(solution)/shard_map/all_gather | solution.py:134
  8.7 250.4 %all-gather.6.cloned.1.call-start = ((), (), s32[]{:S(2)}) async-start(), calls=%async_computation | async-start | bytes 17825792 | tf_op jit(solution)/shard_map/all_gather | solution.py:146
  11.1 289.7 %all-gather.14.cloned.1.call-start = ((), (), s32[]{:S(2)}) async-start(), calls=%async_computation.4 | async-start | bytes 2228224 | tf_op jit(solution)/shard_map/all_gather | solution.py:137
  11.9 3.7 %copy-start.44 = (f32[1,50,32]{1,2,0:T(8,128)S(1)}, f32[1,50,32]{1,2,0:T(8,128)}, u32[]{:S(2)}) copy-start(f32[1,50,32]{1,2,0:T(8,128)} %param.16) | copy-start | bytes 19204
  12.0 6.9 %copy-start.41 = (f32[1024]{0:T(1024)S(1)}, f32[1024]{0:T(1024)}, u32[]{:S(2)}) copy-start(f32[1024]{0:T(1024)} %param.21) | copy-start | bytes 12292
  16.1 117.8 %copy-start.17 = (f32[50,1024]{1,0:T(8,128)}, f32[50,1024]{1,0:T(8,128)S(1)}, u32[]{:S(2)}) copy-start(f32[50,1024]{1,0:T(8,128)S(1)} %get-tuple-element.38) | copy-start | bytes 614404
  17.0 117.0 %copy-start.7 = (f32[50,64]{1,0:T(8,128)}, f32[50,64]{1,0:T(8,128)S(1)}, u32[]{:S(2)}) copy-start(f32[50,64]{1,0:T(8,128)S(1)} %get-tuple-element.33) | copy-start | bytes 38404
  17.0 117.0 %copy-start.12 = (f32[50,64]{1,0:T(8,128)}, f32[50,64]{1,0:T(8,128)S(1)}, u32[]{:S(2)}) copy-start(f32[50,64]{1,0:T(8,128)S(1)} %get-tuple-element.34) | copy-start | bytes 38404
  17.0 252.6 %copy-start.53 = (pred[256]{0:T(512)(128)(4,1)}, pred[256]{0:T(512)(128)(4,1)S(1)}, u32[]{:S(2)}) copy-start(pred[256]{0:T(512)(128)(4,1)S(1)} %iota_compare_fusion) | copy-start | bytes 772
  91.4 167.7 %copy-start.58 = (f32[8192]{0:T(1024)S(1)}, f32[8192]{0:T(1024)}, u32[]{:S(2)}) copy-start(f32[8192]{0:T(1024)} %param.17) | copy-start | bytes 98308
  269.0 1.4 copy-start.39
  269.7 1.1 copy-start.49
  270.1 30.6 %copy-start.18 = (f32[50,1024]{1,0:T(8,128)S(1)}, f32[50,1024]{1,0:T(8,128)}, u32[]{:S(2)}) copy-start(f32[50,1024]{1,0:T(8,128)} %copy-done.17) | copy-start | bytes 614404
  270.8 32.2 %copy-start.30 = (bf16[1024,32]{0,1:T(8,128)(2,1)S(1)}, bf16[1024,32]{0,1:T(8,128)(2,1)}, u32[]{:S(2)}) copy-start(bf16[1024,32]{0,1:T(8,128)(2,1)} %param.27) | copy-start | bytes 196612
  270.8 32.2 %copy-start.45 = (f32[1,50,32]{1,2,0:T(8,128)S(1)}, f32[1,50,32]{1,2,0:T(8,128)}, u32[]{:S(2)}) copy-start(f32[1,50,32]{1,2,0:T(8,128)} %param.16) | copy-start | bytes 19204
  270.8 32.2 %copy-start.46 = (f32[1024]{0:T(1024)S(1)}, f32[1024]{0:T(1024)}, u32[]{:S(2)}) copy-start(f32[1024]{0:T(1024)} %param.26) | copy-start | bytes 12292
  270.8 32.4 %copy-start.52 = (f32[1024]{0:T(1024)S(1)}, f32[1024]{0:T(1024)}, u32[]{:S(2)}) copy-start(f32[1024]{0:T(1024)} %pad_maximum_fusion.2) | copy-start | bytes 12292
  271.1 32.7 %copy-start.42 = (f32[1024]{0:T(1024)S(1)}, f32[1024]{0:T(1024)}, u32[]{:S(2)}) copy-start(f32[1024]{0:T(1024)} %param.21) | copy-start | bytes 12292
  271.1 33.4 %copy-start.1 = (bf16[1024,1024]{1,0:T(8,128)(2,1)S(1)}, bf16[1024,1024]{1,0:T(8,128)(2,1)}, u32[]{:S(2)}) copy-start(bf16[1024,1024]{1,0:T(8,128)(2,1)} %all-gather.8.cloned.1.call-done) | copy-start | bytes 6291460
  303.2 1.8 copy-start.8
  303.2 1.8 copy-start.13
  303.7 0.7 copy-start.21
  304.4 3.2 copy-start.25
  304.4 1.5 copy-start.54
  304.9 2.7 copy-start.4
  305.3 0.7 copy-start.34
  310.2 7.4 %copy-start.3 = (bf16[1024,512]{1,0:T(8,128)(2,1)S(1)}, bf16[1024,512]{1,0:T(8,128)(2,1)}, u32[]{:S(2)}) copy-start(bf16[1024,512]{1,0:T(8,128)(2,1)} %all-gather.12.cloned.1.call-done) | copy-start | bytes 3145732
  310.2 7.4 %copy-start.26 = (bf16[50,1024]{1,0:T(8,128)(2,1)S(1)}, bf16[50,1024]{1,0:T(8,128)(2,1)}, u32[]{:S(2)}) copy-start(bf16[50,1024]{1,0:T(8,128)(2,1)} %copy-done.25) | copy-start | bytes 307204
  313.3 2.0 copy-start.37
  314.1 1.4 copy-start.50
  315.4 2.1 copy-start.57
  323.6 2.3 copy-start.31
  323.6 2.3 copy-start.47
  323.6 2.5 copy-start.51
  323.6 3.7 %copy-start.43 = (f32[1024]{0:T(1024)S(1)}, f32[1024]{0:T(1024)}, u32[]{:S(2)}) copy-start(f32[1024]{0:T(1024)} %param.21) | copy-start | bytes 12292
  326.1 1.9 copy-start.40
  326.2 1.9 copy-start.9
  326.2 1.9 copy-start.14
  326.7 0.7 copy-start.22
  327.4 2.7 copy-start.27
  327.5 1.6 copy-start.55
  327.9 2.2 copy-start.5
  328.4 0.7 copy-start.35
  332.6 6.7 %copy-start.28 = (bf16[50,1024]{1,0:T(8,128)(2,1)S(1)}, bf16[50,1024]{1,0:T(8,128)(2,1)}, u32[]{:S(2)}) copy-start(bf16[50,1024]{1,0:T(8,128)(2,1)} %copy-done.27) | copy-start | bytes 307204
  335.7 1.4 copy-start.38
  345.3 2.2 copy-start.32
  348.5 3.3 copy-start.10
  348.5 3.3 copy-start.15
  349.7 0.7 copy-start.19
  351.2 1.3 copy-start.23
  351.2 0.9 copy-start.56
  351.7 1.2 copy-start.6
  351.8 1.6 copy-start.11
  351.9 1.6 copy-start.16
  353.0 1.2 copy-start.29
  353.3 3.4 copy-start.24
  353.8 0.7 copy-start.36
  354.5 5.5 %copy-start.2 = (bf16[1024,1024]{1,0:T(8,128)(2,1)S(1)}, bf16[1024,1024]{1,0:T(8,128)(2,1)}, u32[]{:S(2)}) copy-start(bf16[1024,1024]{1,0:T(8,128)(2,1)} %all-gather.14.cloned.1.call-done) | copy-start | bytes 6291460
  354.5 5.5 %copy-start.20 = (f32[50,1024]{1,0:T(8,128)S(1)}, f32[50,1024]{1,0:T(8,128)}, u32[]{:S(2)}) copy-start(f32[50,1024]{1,0:T(8,128)} %copy-done.19) | copy-start | bytes 614404
  357.6 2.9 copy-start.33
  357.6 2.9 copy-start.48
Sparse Core Ops, SparseCore 0:
  9.5 40.6 all-gather.9
  52.4 36.8 all-gather.11
  91.4 40.4 all-gather.7
  133.9 125.1 all-gather.5
  261.1 39.6 all-gather.13
where the time goes:
time: 369 us; the launch traced here: 368 us
  waiting for transfers between devices  266 us (72%)
  matrix products  50.5 us (14%)
  local copies, waits for them, and re-layouts  20.1 us (5%)
  other arithmetic  16.4 us (4%)
  between operations  15.1 us (4%)
    all_gather x1, waiting for transfers between devices, shards(): lax.all_gather(stacked, 'wide', axis=1, tiled=True)  124 us
    all_gather x1, waiting for transfers between devices, shards(): lax.all_gather(expert_query, 'wide', axis=0, tiled=True)  40.4 us
    all_gather x1, waiting for transfers between devices, shards(): lax.all_gather(expert_value, 'wide', axis=0, tiled=True)  37.4 us
    all_gather x1, waiting for transfers between devices, shards(): lax.all_gather(expert_key, 'wide', axis=0, tiled=True)  31.2 us
    all_gather x1, waiting for transfers between devices, shards(): lax.all_gather(expert_output, 'wide', axis=0, tiled=True)  29.5 us
    dot_general x1, matrix products, shards(): jnp.einsum('pd,kdc->pkc', normed, lax.all_gather(stacked, 'wide', axis=1,...  9.54 us
  transfers between devices with their start and end apart: 5, of which 5 were waited for; matrix products, arithmetic and copies ran while one was open for 7% of the time, Pallas kernels for 0%

commit v1 on v0

--- a/solution.py
+++ b/solution.py
@@ -140,12 +140,38 @@
     row_count = hidden.shape[0]
     normed = normalize(hidden.astype(jnp.float32), prefix_gain).astype(jnp.bfloat16)
     stacked = jnp.stack([key_weight, value_weight], 0)
-    projected = jnp.einsum(
+    length_2, place, span = (lax.axis_size("wide"), lax.axis_index("wide"), stacked.shape[1])
+    right = [(i, (i + 1) % length_2) for i in range(length_2)]
+    behind = [(i, (i - 1) % length_2) for i in range(length_2)]
+    middle = length_2 // 2
+    from_left = from_right = stacked
+    total = jnp.einsum(
         "pd,kdc->pkc",
-        normed,
-        lax.all_gather(stacked, "wide", axis=1, tiled=True),
+        lax.dynamic_slice_in_dim(normed, place * span, stacked.shape[1], axis=1),
+        stacked,
         preferred_element_type=jnp.float32,
     )
+    for step in range(1, middle + 1):
+        from_left = lax.ppermute(from_left, "wide", right)
+        if step < length_2 - middle:
+            from_right = lax.ppermute(from_right, "wide", behind)
+            total = total + jnp.einsum(
+                "pd,kdc->pkc",
+                lax.dynamic_slice_in_dim(
+                    normed, (place + step) % length_2 * span, from_right.shape[1], axis=1
+                ),
+                from_right,
+                preferred_element_type=jnp.float32,
+            )
+        total = total + jnp.einsum(
+            "pd,kdc->pkc",
+            lax.dynamic_slice_in_dim(
+                normed, (place - step) % length_2 * span, from_left.shape[1], axis=1
+            ),
+            from_left,
+            preferred_element_type=jnp.float32,
+        )
+    projected = total
     positions = jnp.arange(row_count, dtype=jnp.float32)
     key_cache = (
         rotate(projected[:, 0].reshape(row_count, -1, HEAD), positions)

time: 369 us -> 318 us (0.86)
  the two profiles are of different devices: /device:TPU:0 before, /device:TPU:1 now
where the time goes in v1:
time: 318 us; the launch traced here: 317 us
  waiting for transfers between devices  173 us (54%)
  matrix products  64.4 us (20%)
  local copies, waits for them, and re-layouts  25.1 us (8%)
  other arithmetic  20.1 us (6%)
  starting transfers between devices  18.9 us (6%)
  between operations  15.1 us (5%)
    ppermute x8, waiting for transfers between devices, shards(): from_left = lax.ppermute(from_left, 'wide', right)  80.5 us
    ppermute x7, waiting for transfers between devices, shards(): from_right = lax.ppermute(from_right, 'wide', behind)  56.2 us
    all_gather x1, waiting for transfers between devices, shards(): lax.all_gather(expert_query, 'wide', axis=0, tiled=True)  19.6 us
    ppermute x8, starting transfers between devices, shards(): from_left = lax.ppermute(from_left, 'wide', right)  18 us
    all_gather x1, waiting for transfers between devices, shards(): lax.all_gather(expert_value, 'wide', axis=0, tiled=True)  14.8 us
    dot_general x8, matrix products, shards(): jnp.einsum('pd,kdc->pkc', lax.dynamic_slice_in_dim(normed, (place - step)...  11.1 us
    dot_general x4, matrix products, expert_steps(): jnp.dot(attn_mixed, output_w, preferred_element_type=jnp.float32)  8.07 us
    convert_element_type x8, local copies, waits for them, and re-layouts, attend(): return attn_mixed.reshape(span_rows, -1).astype(jnp.bfloat16)  7.03 us
  transfers between devices with their start and end apart: 19, of which 11 were waited for; matrix products, arithmetic and copies ran while one was open for 14% of the time, Pallas kernels for 0%

profile of v1, /device:TPU:1, one launch (start us, length us, event | category | flops | bytes accessed | tf_op | source)
XLA Modules:
  0.0 316.7 jit_solution(9807925506747875978)
XLA Ops:
  8.8 1.3 pad_maximum_fusion
  10.2 2.7 collective-permute-start.1
  12.9 3.3 %fusion = f32[256]{0:T(256)S(1)} fusion(bf16[1,256,8192]{2,1,0:T(8,128)(2,1)} %param.14), kind=kLoop, calls=%fused_computation.2 | loop fusion | flops 6291200 | bytes 4195328 | tf_op jit(solution)/shard_map/reduce_sum | solution.py:13
  16.3 3.2 fusion.2
  20.2 16.3 %collective-permute-done.1 = bf16[2,512,512]{2,1,0:T(8,128)(2,1)} collective-permute-done((bf16[2,512,512]{2,1,0:T(8,128)(2,1)S(1)}, bf16[2,512,512]{2,1,0:T(8,128)(2,1)}, u32[]{:S(2)}, u32[]{:S(2)}) %collective-permute-start.1) | collective-permute-done | bytes 1048608 | tf_op jit(solution)/shard_map/ppermute | solution.py:155
  36.5 2.6 collective-permute-start.3
  41.7 23.5 %collective-permute-done.3 = bf16[2,512,512]{2,1,0:T(8,128)(2,1)S(1)} collective-permute-done((bf16[2,512,512]{2,1,0:T(8,128)(2,1)}, bf16[2,512,512]{2,1,0:T(8,128)(2,1)S(1)}, u32[]{:S(2)}, u32[]{:S(2)}) %collective-permute-start.3) | collective-permute-done | bytes 1048608 | tf_op jit(solution)/shard_map/ppermute | solution.py:155
  65.2 2.4 collective-permute-start.5
  67.6 1.7 fusion.51
  69.5 1.2 fusion.86
  70.8 4.6 %collective-permute-done.2 = bf16[2,512,512]{2,1,0:T(8,128)(2,1)S(1)} collective-permute-done((bf16[2,512,512]{2,1,0:T(8,128)(2,1)S(1)}, bf16[2,512,512]{2,1,0:T(8,128)(2,1)S(1)}, u32[]{:S(2)}, u32[]{:S(2)}) %collective-permute-start.2) | collective-permute-done | bytes 1048608 | tf_op jit(solution)/shard_map/ppermute | solution.py:157
  75.4 15.8 %collective-permute-done.5 = bf16[2,512,512]{2,1,0:T(8,128)(2,1)} collective-permute-done((bf16[2,512,512]{2,1,0:T(8,128)(2,1)S(1)}, bf16[2,512,512]{2,1,0:T(8,128)(2,1)}, u32[]{:S(2)}, u32[]{:S(2)}) %collective-permute-start.5) | collective-permute-done | bytes 1048608 | tf_op jit(solution)/shard_map/ppermute | solution.py:155
  91.3 2.6 collective-permute-start.7
  93.9 1.4 convolution_add_fusion.8
  95.2 1.8 convolution_add_fusion.7
  97.0 1.5 fusion.162
  98.6 14.8 %all-gather.9.cloned.1.call-done = bf16[1024,512]{1,0:T(8,128)(2,1)} async-done(((bf16[64,512]{1,0:T(8,128)(2,1)}), bf16[1024,512]{1,0:T(8,128)(2,1)}) %all-gather.9.cloned.1.call-update) | async-done | bytes 1048592 | tf_op jit(solution)/shard_map/all_gather | solution.py:136
  113.3 1.5 convolution_convert_fusion.3
  115.9 1.5 collective-permute-start.9
  118.1 1.7 fusion.46
  119.8 1.4 fusion.8
  121.2 21.4 %collective-permute-done.6 = bf16[2,512,512]{2,1,0:T(8,128)(2,1)S(1)} collective-permute-done((bf16[2,512,512]{2,1,0:T(8,128)(2,1)}, bf16[2,512,512]{2,1,0:T(8,128)(2,1)S(1)}, u32[]{:S(2)}, u32[]{:S(2)}) %collective-permute-start.6) | collective-permute-done | bytes 1048608 | tf_op jit(solution)/shard_map/ppermute | solution.py:157
  142.6 1.7 fusion.43
  144.3 9.0 %collective-permute-done.9 = bf16[2,512,512]{2,1,0:T(8,128)(2,1)} collective-permute-done((bf16[2,512,512]{2,1,0:T(8,128)(2,1)}, bf16[2,512,512]{2,1,0:T(8,128)(2,1)}, u32[]{:S(2)}, u32[]{:S(2)}) %collective-permute-start.9) | collective-permute-done | bytes 1048608 | tf_op jit(solution)/shard_map/ppermute | solution.py:155
  153.4 2.5 collective-permute-start.11
  155.8 1.8 fusion.7
  157.6 19.6 %all-gather.5.cloned.1.call-done = bf16[1024,1024]{1,0:T(8,128)(2,1)} async-done(((bf16[64,1024]{1,0:T(8,128)(2,1)}), bf16[1024,1024]{1,0:T(8,128)(2,1)}) %all-gather.5.cloned.1.call-update) | async-done | bytes 2097168 | tf_op jit(solution)/shard_map/all_gather | solution.py:134
  177.2 2.2 fusion.161
  181.1 1.5 collective-permute-start.13
  182.6 1.7 fusion.40
  184.7 1.7 fusion.37
  186.4 20.3 %collective-permute-done.10 = bf16[2,512,512]{2,1,0:T(8,128)(2,1)S(1)} collective-permute-done((bf16[2,512,512]{2,1,0:T(8,128)(2,1)S(1)}, bf16[2,512,512]{2,1,0:T(8,128)(2,1)S(1)}, u32[]{:S(2)}, u32[]{:S(2)}) %collective-permute-start.10) | collective-permute-done | bytes 1048608 | tf_op jit(solution)/shard_map/ppermute | solution.py:157
  207.2 15.8 %collective-permute-done.13 = bf16[2,512,512]{2,1,0:T(8,128)(2,1)S(1)} collective-permute-done((bf16[2,512,512]{2,1,0:T(8,128)(2,1)}, bf16[2,512,512]{2,1,0:T(8,128)(2,1)S(1)}, u32[]{:S(2)}, u32[]{:S(2)}) %collective-permute-start.13) | collective-permute-done | bytes 1048608 | tf_op jit(solution)/shard_map/ppermute | solution.py:155
  223.0 2.4 collective-permute-start.14
  225.4 1.7 fusion.34
  227.9 9.9 %collective-permute-done.12 = bf16[2,512,512]{2,1,0:T(8,128)(2,1)S(1)} collective-permute-done((bf16[2,512,512]{2,1,0:T(8,128)(2,1)S(1)}, bf16[2,512,512]{2,1,0:T(8,128)(2,1)S(1)}, u32[]{:S(2)}, u32[]{:S(2)}) %collective-permute-start.12) | collective-permute-done | bytes 1048608 | tf_op jit(solution)/shard_map/ppermute | solution.py:157
  242.6 1.6 convert_element_type.164
  244.2 2.2 multiply_reduce_fusion.6
  246.4 1.1 fusion.25
  247.4 1.2 multiply_reduce_fusion.5
  252.8 1.5 fusion.163
  260.6 1.5 reshape.312
  262.0 1.3 fusion.19
  264.1 1.6 convert_element_type.174
  265.6 2.2 multiply_reduce_fusion.4
  267.8 1.1 fusion.24
  269.0 1.2 multiply_reduce_fusion.3
  272.3 2.1 fusion.166
  274.4 1.6 reshape.314
  276.0 1.1 fusion.150
  277.1 1.4 fusion.165
  279.7 1.1 fusion.157
  284.1 1.5 reshape.315
  285.5 1.3 fusion.18
  287.6 1.6 convert_element_type.184
  289.2 2.2 multiply_reduce_fusion.2
  291.4 1.1 fusion.23
  292.4 1.2 multiply_reduce_fusion.1
  295.8 2.2 fusion.168
  297.9 1.6 reshape.317
  299.5 1.1 fusion.149
  300.6 1.4 fusion.167
  306.3 1.3 fusion.17
  307.8 1.5 multiply_reduce_fusion
  (228 shorter events, 40.4 us)
Async XLA Ops:
  6.5 34.6 %copy-start = (f32[32,1024]{1,0:T(8,128)S(1)}, f32[32,1024]{1,0:T(8,128)}, u32[]{:S(2)}) copy-start(f32[32,1024]{1,0:T(8,128)} %param.20) | copy-start | bytes 393220
  6.5 9.6 %copy-start.45 = (f32[8192]{0:T(1024)S(1)}, f32[8192]{0:T(1024)}, u32[]{:S(2)}) copy-start(f32[8192]{0:T(1024)} %param.17) | copy-start | bytes 98308
  6.5 90.5 %all-gather.7.cloned.1.call-start = ((), (), s32[]{:S(2)}) async-start(), calls=%async_computation.1 | async-start | bytes 1114112 | tf_op jit(solution)/shard_map/all_gather | solution.py:135
  7.3 106.1 %all-gather.9.cloned.1.call-start = ((), (), s32[]{:S(2)}) async-start(), calls=%async_computation.2 | async-start | bytes 1114112 | tf_op jit(solution)/shard_map/all_gather | solution.py:136
  8.0 169.2 %all-gather.5.cloned.1.call-start = ((), (), s32[]{:S(2)}) async-start(), calls=%async_computation | async-start | bytes 2228224 | tf_op jit(solution)/shard_map/all_gather | solution.py:134
  8.7 235.4 %all-gather.11.cloned.1.call-start = ((), (), s32[]{:S(2)}) async-start(), calls=%async_computation.3 | async-start | bytes 2228224 | tf_op jit(solution)/shard_map/all_gather | solution.py:137
  10.1 31.5 %collective-permute-start = (bf16[2,512,512]{2,1,0:T(8,128)(2,1)S(1)}, bf16[2,512,512]{2,1,0:T(8,128)(2,1)S(1)}, u32[]{:S(2)}, u32[]{:S(2)}) collective-permute-start(bf16[2,512,512]{2,1,0:T(8,128)(2,1)S(1)} %pad_maximum_fusion), channel_id=1, source_target_pairs={{0,15},{1,0},{2,1},{3,2},{4,3},{5,4},{6,5},{7,6},{8,7},{9,8},{10,9... | collective-permute-start | bytes 3145736 | tf_op jit(solution)/shard_map/ppermute | solution.py:157
  10.2 26.3 %collective-permute-start.1 = (bf16[2,512,512]{2,1,0:T(8,128)(2,1)S(1)}, bf16[2,512,512]{2,1,0:T(8,128)(2,1)}, u32[]{:S(2)}, u32[]{:S(2)}) collective-permute-start(bf16[2,512,512]{2,1,0:T(8,128)(2,1)S(1)} %pad_maximum_fusion), channel_id=1, source_target_pairs={{0,1},{1,2},{2,3},{3,4},{4,5},{5,6},{6,7},{7,8},{8,9},{9,10},{10,1... | collective-permute-start | bytes 3145736 | tf_op jit(solution)/shard_map/ppermute | solution.py:155
  12.9 3.5 %copy-start.5 = (bf16[1,256,8192]{2,1,0:T(8,128)(2,1)S(1)}, bf16[1,256,8192]{2,1,0:T(8,128)(2,1)}, u32[]{:S(2)}) copy-start(bf16[1,256,8192]{2,1,0:T(8,128)(2,1)} %param.14) | copy-start | bytes 12582916
  16.3 24.8 %copy-start.41 = (f32[1,50,32]{1,2,0:T(8,128)S(1)}, f32[1,50,32]{1,2,0:T(8,128)}, u32[]{:S(2)}) copy-start(f32[1,50,32]{1,2,0:T(8,128)} %param.16) | copy-start | bytes 19204
  16.3 54.4 %copy-start.40 = (f32[1024]{0:T(1024)S(1)}, f32[1024]{0:T(1024)}, u32[]{:S(2)}) copy-start(f32[1024]{0:T(1024)} %param.21) | copy-start | bytes 12292
  36.5 28.7 %collective-permute-start.3 = (bf16[2,512,512]{2,1,0:T(8,128)(2,1)}, bf16[2,512,512]{2,1,0:T(8,128)(2,1)S(1)}, u32[]{:S(2)}, u32[]{:S(2)}) collective-permute-start(bf16[2,512,512]{2,1,0:T(8,128)(2,1)} %collective-permute-done.1), channel_id=1, source_target_pairs={{0,1},{1,2},{2,3},{3,4},{4,5},{5,6},{6,7},{7,8},{8,9},{9,10},{10,1... | collective-permute-start | bytes 3145736 | tf_op jit(solution)/shard_map/ppermute | solution.py:155
  39.1 201.4 %copy-start.46 = (pred[256]{0:T(512)(128)(4,1)}, pred[256]{0:T(512)(128)(4,1)S(1)}, u32[]{:S(2)}) copy-start(pred[256]{0:T(512)(128)(4,1)S(1)} %iota_compare_fusion) | copy-start | bytes 772
  41.6 49.7 %copy-start.13 = (f32[50,1024]{1,0:T(8,128)}, f32[50,1024]{1,0:T(8,128)S(1)}, u32[]{:S(2)}) copy-start(f32[50,1024]{1,0:T(8,128)S(1)} %get-tuple-element.38) | copy-start | bytes 614404
  41.6 33.8 %collective-permute-start.2 = (bf16[2,512,512]{2,1,0:T(8,128)(2,1)S(1)}, bf16[2,512,512]{2,1,0:T(8,128)(2,1)S(1)}, u32[]{:S(2)}, u32[]{:S(2)}) collective-permute-start(bf16[2,512,512]{2,1,0:T(8,128)(2,1)S(1)} %collective-permute-done), channel_id=1, source_target_pairs={{0,15},{1,0},{2,1},{3,2},{4,3},{5,4},{6,5},{7,6},{8,7},{9,8},{10,9... | collective-permute-start | bytes 3145736 | tf_op jit(solution)/shard_map/ppermute | solution.py:157
  65.2 28.6 %copy-start.23 = (bf16[2,512,512]{2,1,0:T(8,128)(2,1)}, bf16[2,512,512]{2,1,0:T(8,128)(2,1)S(1)}, u32[]{:S(2)}) copy-start(bf16[2,512,512]{2,1,0:T(8,128)(2,1)S(1)} %collective-permute-done.3) | copy-start | bytes 3145732
  65.2 26.1 %collective-permute-start.5 = (bf16[2,512,512]{2,1,0:T(8,128)(2,1)S(1)}, bf16[2,512,512]{2,1,0:T(8,128)(2,1)}, u32[]{:S(2)}, u32[]{:S(2)}) collective-permute-start(bf16[2,512,512]{2,1,0:T(8,128)(2,1)S(1)} %collective-permute-done.3), channel_id=1, source_target_pairs={{0,1},{1,2},{2,3},{3,4},{4,5},{5,6},{6,7},{7,8},{8,9},{9,10},{10,1... | collective-permute-start | bytes 3145736 | tf_op jit(solution)/shard_map/ppermute | solution.py:155
  69.5 110.0 %copy-start.7 = (f32[50,64]{1,0:T(8,128)}, f32[50,64]{1,0:T(8,128)S(1)}, u32[]{:S(2)}) copy-start(f32[50,64]{1,0:T(8,128)S(1)} %get-tuple-element.33) | copy-start | bytes 38404
  69.5 110.0 %copy-start.10 = (f32[50,64]{1,0:T(8,128)}, f32[50,64]{1,0:T(8,128)S(1)}, u32[]{:S(2)}) copy-start(f32[50,64]{1,0:T(8,128)S(1)} %get-tuple-element.34) | copy-start | bytes 38404
  75.4 40.1 %collective-permute-start.4 = (bf16[2,512,512]{2,1,0:T(8,128)(2,1)S(1)}, bf16[2,512,512]{2,1,0:T(8,128)(2,1)}, u32[]{:S(2)}, u32[]{:S(2)}) collective-permute-start(bf16[2,512,512]{2,1,0:T(8,128)(2,1)S(1)} %collective-permute-done.2), channel_id=1, source_target_pairs={{0,15},{1,0},{2,1},{3,2},{4,3},{5,4},{6,5},{7,6},{8,7},{9,8},{10,9... | collective-permute-start | bytes 3145736 | tf_op jit(solution)/shard_map/ppermute | solution.py:157
  91.3 24.7 %collective-permute-start.7 = (bf16[2,512,512]{2,1,0:T(8,128)(2,1)}, bf16[2,512,512]{2,1,0:T(8,128)(2,1)}, u32[]{:S(2)}, u32[]{:S(2)}) collective-permute-start(bf16[2,512,512]{2,1,0:T(8,128)(2,1)} %collective-permute-done.5), channel_id=1, source_target_pairs={{0,1},{1,2},{2,3},{3,4},{4,5},{5,6},{6,7},{7,8},{8,9},{9,10},{10,1... | collective-permute-start | bytes 3145736 | tf_op jit(solution)/shard_map/ppermute | solution.py:155
  115.5 27.1 %collective-permute-start.6 = (bf16[2,512,512]{2,1,0:T(8,128)(2,1)}, bf16[2,512,512]{2,1,0:T(8,128)(2,1)S(1)}, u32[]{:S(2)}, u32[]{:S(2)}) collective-permute-start(bf16[2,512,512]{2,1,0:T(8,128)(2,1)} %collective-permute-done.4), channel_id=1, source_target_pairs={{0,15},{1,0},{2,1},{3,2},{4,3},{5,4},{6,5},{7,6},{8,7},{9,8},{10,9... | collective-permute-start | bytes 3145736 | tf_op jit(solution)/shard_map/ppermute | solution.py:157
  115.9 37.4 %collective-permute-start.9 = (bf16[2,512,512]{2,1,0:T(8,128)(2,1)}, bf16[2,512,512]{2,1,0:T(8,128)(2,1)}, u32[]{:S(2)}, u32[]{:S(2)}) collective-permute-start(bf16[2,512,512]{2,1,0:T(8,128)(2,1)} %collective-permute-done.7), channel_id=1, source_target_pairs={{0,1},{1,2},{2,3},{3,4},{4,5},{5,6},{6,7},{7,8},{8,9},{9,10},{10,1... | collective-permute-start | bytes 3145736 | tf_op jit(solution)/shard_map/ppermute | solution.py:155
  142.6 37.2 %collective-permute-start.8 = (bf16[2,512,512]{2,1,0:T(8,128)(2,1)S(1)}, bf16[2,512,512]{2,1,0:T(8,128)(2,1)S(1)}, u32[]{:S(2)}, u32[]{:S(2)}) collective-permute-start(bf16[2,512,512]{2,1,0:T(8,128)(2,1)S(1)} %collective-permute-done.6), channel_id=1, source_target_pairs={{0,15},{1,0},{2,1},{3,2},{4,3},{5,4},{6,5},{7,6},{8,7},{9,8},{10,9... | collective-permute-start | bytes 3145736 | tf_op jit(solution)/shard_map/ppermute | solution.py:157
  153.4 27.8 %collective-permute-start.11 = (bf16[2,512,512]{2,1,0:T(8,128)(2,1)}, bf16[2,512,512]{2,1,0:T(8,128)(2,1)}, u32[]{:S(2)}, u32[]{:S(2)}) collective-permute-start(bf16[2,512,512]{2,1,0:T(8,128)(2,1)} %collective-permute-done.9), channel_id=1, source_target_pairs={{0,1},{1,2},{2,3},{3,4},{4,5},{5,6},{6,7},{7,8},{8,9},{9,10},{10,1... | collective-permute-start | bytes 3145736 | tf_op jit(solution)/shard_map/ppermute | solution.py:155
  177.2 3.0 copy-start.38
  177.2 5.4 %copy-start.6 = (bf16[256,8192]{1,0:T(8,128)(2,1)S(1)}, bf16[256,8192]{1,0:T(8,128)(2,1)}, u32[]{:S(2)}) copy-start(bf16[256,8192]{1,0:T(8,128)(2,1)} %fusion.2) | copy-start | bytes 12582916
  179.8 6.6 %copy-start.25 = (bf16[50,8,128]{2,0,1:T(8,128)(2,1)}, bf16[50,8,128]{2,0,1:T(8,128)(2,1)S(1)}, u32[]{:S(2)}) copy-start(bf16[50,8,128]{2,0,1:T(8,128)(2,1)S(1)} %copy.37) | copy-start | bytes 307204
  179.8 26.9 %collective-permute-start.10 = (bf16[2,512,512]{2,1,0:T(8,128)(2,1)S(1)}, bf16[2,512,512]{2,1,0:T(8,128)(2,1)S(1)}, u32[]{:S(2)}, u32[]{:S(2)}) collective-permute-start(bf16[2,512,512]{2,1,0:T(8,128)(2,1)S(1)} %collective-permute-done.8), channel_id=1, source_target_pairs={{0,15},{1,0},{2,1},{3,2},{4,3},{5,4},{6,5},{7,6},{8,7},{9,8},{10,9... | collective-permute-start | bytes 3145736 | tf_op jit(solution)/shard_map/ppermute | solution.py:157
  181.1 41.8 %collective-permute-start.13 = (bf16[2,512,512]{2,1,0:T(8,128)(2,1)}, bf16[2,512,512]{2,1,0:T(8,128)(2,1)S(1)}, u32[]{:S(2)}, u32[]{:S(2)}) collective-permute-start(bf16[2,512,512]{2,1,0:T(8,128)(2,1)} %collective-permute-done.11), channel_id=1, source_target_pairs={{0,1},{1,2},{2,3},{3,4},{4,5},{5,6},{6,7},{7,8},{8,9},{9,10},{10,1... | collective-permute-start | bytes 3145736 | tf_op jit(solution)/shard_map/ppermute | solution.py:155
  206.8 31.1 %collective-permute-start.12 = (bf16[2,512,512]{2,1,0:T(8,128)(2,1)S(1)}, bf16[2,512,512]{2,1,0:T(8,128)(2,1)S(1)}, u32[]{:S(2)}, u32[]{:S(2)}) collective-permute-start(bf16[2,512,512]{2,1,0:T(8,128)(2,1)S(1)} %collective-permute-done.10), channel_id=1, source_target_pairs={{0,15},{1,0},{2,1},{3,2},{4,3},{5,4},{6,5},{7,6},{8,7},{9,8},{10,9... | collective-permute-start | bytes 3145736 | tf_op jit(solution)/shard_map/ppermute | solution.py:157
  223.0 15.3 %collective-permute-start.14 = (bf16[2,512,512]{2,1,0:T(8,128)(2,1)S(1)}, bf16[2,512,512]{2,1,0:T(8,128)(2,1)S(1)}, u32[]{:S(2)}, u32[]{:S(2)}) collective-permute-start(bf16[2,512,512]{2,1,0:T(8,128)(2,1)S(1)} %collective-permute-done.13), channel_id=1, source_target_pairs={{0,1},{1,2},{2,3},{3,4},{4,5},{5,6},{6,7},{7,8},{8,9},{9,10},{10,1... | collective-permute-start | bytes 3145736 | tf_op jit(solution)/shard_map/ppermute | solution.py:155
  238.3 1.9 copy-start.32
  238.3 1.9 copy-start.33
  238.7 1.7 copy-start.26
  238.8 2.1 copy-start.27
  239.8 1.5 copy-start.34
  239.8 1.8 copy-start.28
  239.8 1.8 copy-start.43
  240.9 9.9 %copy-start.4 = (bf16[1024,512]{1,0:T(8,128)(2,1)S(1)}, bf16[1024,512]{1,0:T(8,128)(2,1)}, u32[]{:S(2)}) copy-start(bf16[1024,512]{1,0:T(8,128)(2,1)} %all-gather.7.cloned.1.call-done) | copy-start | bytes 3145732
  241.3 11.5 %copy-start.1 = (bf16[1024,1024]{1,0:T(8,128)(2,1)S(1)}, bf16[1024,1024]{1,0:T(8,128)(2,1)}, u32[]{:S(2)}) copy-start(bf16[1024,1024]{1,0:T(8,128)(2,1)} %all-gather.5.cloned.1.call-done) | copy-start | bytes 6291460
  248.6 0.7 copy-start.15
  252.6 5.9 %copy-start.35 = (bf16[256,4,128]{2,1,0:T(4,128)(2,1)S(1)}, bf16[256,4,128]{2,1,0:T(4,128)(2,1)}, u32[]{:S(2)}) copy-start(bf16[256,4,128]{2,1,0:T(4,128)(2,1)} %convert_element_type.154) | copy-start | bytes 786436
  252.8 6.9 %copy-start.3 = (bf16[1024,512]{1,0:T(8,128)(2,1)S(1)}, bf16[1024,512]{1,0:T(8,128)(2,1)}, u32[]{:S(2)}) copy-start(bf16[1024,512]{1,0:T(8,128)(2,1)} %all-gather.9.cloned.1.call-done) | copy-start | bytes 3145732
  252.8 6.9 %copy-start.20 = (bf16[50,1024]{1,0:T(8,128)(2,1)S(1)}, bf16[50,1024]{1,0:T(8,128)(2,1)}, u32[]{:S(2)}) copy-start(bf16[50,1024]{1,0:T(8,128)(2,1)} %copy-done.19) | copy-start | bytes 307204
  257.5 0.7 copy-start.30
  257.6 2.1 copy-start.44
  258.6 1.0 copy-start.48
  268.9 1.2 copy-start.39
  270.1 0.7 copy-start.16
  276.0 4.8 %copy-start.8 = (f32[50,64]{1,0:T(8,128)S(1)}, f32[50,64]{1,0:T(8,128)}, u32[]{:S(2)}) copy-start(f32[50,64]{1,0:T(8,128)} %copy-done.7) | copy-start | bytes 38404
  276.0 4.8 %copy-start.11 = (f32[50,64]{1,0:T(8,128)S(1)}, f32[50,64]{1,0:T(8,128)}, u32[]{:S(2)}) copy-start(f32[50,64]{1,0:T(8,128)} %copy-done.10) | copy-start | bytes 38404
  276.0 6.1 %copy-start.36 = (bf16[256,4,128]{2,1,0:T(4,128)(2,1)S(1)}, bf16[256,4,128]{2,1,0:T(4,128)(2,1)}, u32[]{:S(2)}) copy-start(bf16[256,4,128]{2,1,0:T(4,128)(2,1)} %convert_element_type.154) | copy-start | bytes 786436
  277.1 6.1 %copy-start.22 = (bf16[50,1024]{1,0:T(8,128)(2,1)S(1)}, bf16[50,1024]{1,0:T(8,128)(2,1)}, u32[]{:S(2)}) copy-start(bf16[50,1024]{1,0:T(8,128)(2,1)} %copy-done.21) | copy-start | bytes 307204
  281.1 0.7 copy-start.31
  293.6 0.7 copy-start.14
  299.5 3.7 %copy-start.47 = (pred[256]{0:T(512)(128)(4,1)S(1)}, pred[256]{0:T(512)(128)(4,1)}, u32[]{:S(2)}) copy-start(pred[256]{0:T(512)(128)(4,1)} %copy-done.46) | copy-start | bytes 772
  299.5 4.1 %copy-start.9 = (f32[50,64]{1,0:T(8,128)S(1)}, f32[50,64]{1,0:T(8,128)}, u32[]{:S(2)}) copy-start(f32[50,64]{1,0:T(8,128)} %copy-done.7) | copy-start | bytes 38404
  299.5 4.1 %copy-start.12 = (f32[50,64]{1,0:T(8,128)S(1)}, f32[50,64]{1,0:T(8,128)}, u32[]{:S(2)}) copy-start(f32[50,64]{1,0:T(8,128)} %copy-done.10) | copy-start | bytes 38404
  299.5 5.5 %copy-start.37 = (bf16[256,4,128]{2,1,0:T(4,128)(2,1)S(1)}, bf16[256,4,128]{2,1,0:T(4,128)(2,1)}, u32[]{:S(2)}) copy-start(bf16[256,4,128]{2,1,0:T(4,128)(2,1)} %convert_element_type.154) | copy-start | bytes 786436
  300.6 5.4 %copy-start.18 = (bf16[50,1024]{1,0:T(8,128)(2,1)S(1)}, bf16[50,1024]{1,0:T(8,128)(2,1)}, u32[]{:S(2)}) copy-start(bf16[50,1024]{1,0:T(8,128)(2,1)} %copy-done.17) | copy-start | bytes 307204
  303.0 4.7 %copy-start.2 = (bf16[1024,1024]{1,0:T(8,128)(2,1)S(1)}, bf16[1024,1024]{1,0:T(8,128)(2,1)}, u32[]{:S(2)}) copy-start(bf16[1024,1024]{1,0:T(8,128)(2,1)} %all-gather.11.cloned.1.call-done) | copy-start | bytes 6291460
  304.6 4.7 %copy-start.24 = (bf16[1024,32]{0,1:T(8,128)(2,1)S(1)}, bf16[1024,32]{0,1:T(8,128)(2,1)}, u32[]{:S(2)}) copy-start(bf16[1024,32]{0,1:T(8,128)(2,1)} %param.27) | copy-start | bytes 196612
  304.6 4.7 %copy-start.42 = (f32[1024]{0:T(1024)S(1)}, f32[1024]{0:T(1024)}, u32[]{:S(2)}) copy-start(f32[1024]{0:T(1024)} %param.26) | copy-start | bytes 12292
  (4 other events, 2.6 us)
Sparse Core Ops, SparseCore 0:
  9.5 57.6 all-gather.6
  69.3 43.9 all-gather.8
  115.5 61.6 all-gather.4
  179.2 57.2 all-gather.10
